TPU v7x, 32 devices: a whole 2x2x4 slice. The times are simulated.
32 devices in a mesh: dp: 8 (over z, core), fsdp: 4 (over y, x).
Axes of the slice: x: 2, y: 2, z: 4, core: 2. Of those that a mesh axis runs over, the one named last changes fastest.
Arguments:
- old_weight: float32 [8192, 1024], P('dp', 'fsdp'), may hold values from -6 to 6
- old_first: float32 [8192, 1024], P('dp', 'fsdp'), may hold values from -6 to 6
- old_second: float32 [8192, 1024], P('dp', 'fsdp'), may hold values from 0.01 to 1
- grads: bfloat16 [8, 8, 1024, 1024], P('dp', None, 'fsdp'), may hold values from -60 to 60
- column_shard_lookup: int32 [8, 4], P('dp'), may hold values from 0 to 3, each once within a row
- alive: int32 [8], replicated, may hold values from 0 to 1, as said below
Outputs:
- new_weight: float32 [8192, 1024], P(('dp', 'fsdp'))
- new_first: float32 [8192, 1024], P(('dp', 'fsdp'))
- second_moment_next: float32 [8192, 1024], P(('dp', 'fsdp'))
Inputs may be any that keep to these rules, and one draw needn't show every extreme that they name: `column_shard_lookup`: each row is a permutation of 0 to 3. `alive`: at least 4 entries are 1 and at least one is 0.
All inputs are finite; a program needn't handle non-finite values.
Results may differ from a plain program's by a relative error of at most 0.0003.
Values sent between devices are 32-bit elements; how exact they have to be, the bound alone decides.
A program may use at most 64 MiB of HBM per device.

v0:
```python
import jax
import jax.numpy as jnp
from jax import lax
from jax.sharding import PartitionSpec as P

STEP = 1000


def restore_columns(block, column_order, shards):
    rows_here = block.shape[0]
    pieces = block.reshape(rows_here, shards, block.shape[1] // shards)
    return jnp.take(pieces, column_order, axis=1).reshape(rows_here, block.shape[1])


def body(old_weight, old_first, old_second, grads, column_shard_lookup, alive):
    shards = lax.axis_size("fsdp")
    arrived = (
        lax.all_to_all(old_weight, "fsdp", split_axis=0, concat_axis=1, tiled=True),
        lax.all_to_all(old_first, "fsdp", split_axis=0, concat_axis=1, tiled=True),
        lax.all_to_all(old_second, "fsdp", split_axis=0, concat_axis=1, tiled=True),
    )
    column_order = jnp.argsort(column_shard_lookup[0])
    weight = restore_columns(arrived[0], column_order, shards)
    first = restore_columns(arrived[1], column_order, shards)
    second = restore_columns(arrived[2], column_order, shards)
    live_mask = alive.astype(jnp.float32)
    remaining_entries = jnp.sum(live_mask)
    own_live = lax.dynamic_index_in_dim(live_mask, lax.axis_index("dp"), 0, keepdims=False)
    partial_grad = grads[0]
    masked = partial_grad.astype(jnp.float32) * own_live
    reduced_total = lax.psum_scatter(masked, "dp", scatter_dimension=0, tiled=True)
    gradient_matrix = reduced_total[0] / remaining_entries
    first_new = 0.9 * first + 0.1 * gradient_matrix
    second_new = 0.95 * second + 0.05 * gradient_matrix * gradient_matrix
    first_hat = first_new / (1.0 - 0.9**STEP)
    second_corrected = second_new / (1.0 - 0.95**STEP)
    weight_new = weight - 0.02 * (first_hat / (jnp.sqrt(second_corrected) + 1e-08) + 0.25 * weight)
    return (weight_new, first_new, second_new)


def solution(mesh):
    return jax.shard_map(
        body,
        mesh=mesh,
        in_specs=(
            P("dp", "fsdp"),
            P("dp", "fsdp"),
            P("dp", "fsdp"),
            P("dp", None, "fsdp", None),
            P("dp", None),
            P(),
        ),
        out_specs=(P(("dp", "fsdp"), None), P(("dp", "fsdp"), None), P(("dp", "fsdp"), None)),
        check_vma=False,
    )
```

profile of v0, /device:TPU:0, one launch (start us, length us, event | category | flops | bytes accessed | tf_op | source)
XLA Modules:
  0.0 131.0 jit_solution(2045798307776239665)
XLA Ops:
  7.2 0.0 copy-start.2
  7.2 0.0 reduce-scatter.2.cloned.1.call-start
  7.2 6.5 %copy.11 = bf16[1,8,256,1024]{2,3,1,0:T(8,128)(2,1)} copy(bf16[1,8,256,1024]{3,2,1,0:T(8,128)(2,1)} %param.11) | data formatting | bytes 8388608 | tf_op args[3]
  13.7 0.0 copy-done.2
  13.7 0.6 dynamic_slice.4
  14.3 0.0 copy-start
  14.3 6.9 %multiply_bitcast_fusion = f32[8,256,1024]{1,2,0:T(8,128)} fusion(bf16[1,8,256,1024]{2,3,1,0:T(8,128)(2,1)} %copy.11, f32[]{:T(128)} %bitcast.9), kind=kLoop, calls=%fused_computation.3 | loop fusion | flops 4194304 | bytes 12582916 | tf_op jit(solution)/shard_map/mul | solution.py:30
  21.2 0.0 copy-start.1
  21.2 0.0 reduce-scatter.2.cloned.1.call-update
  21.3 0.0 copy-done
  21.3 19.1 %all_to_all.48 = f32[4,256,256]{2,1,0:T(8,128)S(1)} all-to-all(f32[4,256,256]{2,1,0:T(8,128)S(1)} %bitcast.40), channel_id=1, replica_groups=mesh['dp'=8,'fsdp'=4] {'fsdp'}, dimensions={0} | all-to-all | bytes 2097152 | tf_op jit(solution)/shard_map/all_to_all | solution.py:18
  40.4 3.5 %all-to-all-start.1 = ((f32[4,256,256]{2,1,0:T(8,128)}), f32[4,256,256]{2,1,0:T(8,128)S(1)}, u32[]{:S(2)}, u32[]{:S(2)}) async-start(f32[4,256,256]{2,1,0:T(8,128)} %bitcast.5), calls=%async_computation.1 | async-start | bytes 2097152 | tf_op jit(solution)/shard_map/all_to_all | solution.py:19
  43.9 0.0 copy-done.1
  43.9 0.7 sort.17
  44.7 0.6 convert_reduce_fusion
  45.3 11.1 %all-to-all-done.1 = f32[4,256,256]{2,1,0:T(8,128)S(1)} async-done(((f32[4,256,256]{2,1,0:T(8,128)}), f32[4,256,256]{2,1,0:T(8,128)S(1)}, u32[]{:S(2)}, u32[]{:S(2)}) %all-to-all-start.1) | async-done | bytes 1048608 | tf_op jit(solution)/shard_map/all_to_all | solution.py:19
  56.4 4.2 %all-to-all-start.2 = ((f32[4,256,256]{2,1,0:T(8,128)}), f32[4,256,256]{2,1,0:T(8,128)}, u32[]{:S(2)}, u32[]{:S(2)}) async-start(f32[4,256,256]{2,1,0:T(8,128)} %bitcast.12), calls=%async_computation.3 | async-start | bytes 2097152 | tf_op jit(solution)/shard_map/all_to_all | solution.py:20
  60.7 0.6 gather_fusion
  61.3 0.2 select_bitcast_fusion
  61.5 1.3 copy.9
  62.8 0.6 gather_fusion.1
  63.5 10.5 %all-to-all-done.2 = f32[4,256,256]{2,1,0:T(8,128)} async-done(((f32[4,256,256]{2,1,0:T(8,128)}), f32[4,256,256]{2,1,0:T(8,128)}, u32[]{:S(2)}, u32[]{:S(2)}) %all-to-all-start.2) | async-done | bytes 1048608 | tf_op jit(solution)/shard_map/all_to_all | solution.py:20
  74.0 1.9 %gather_fusion.2 = f32[4,256,256]{2,1,0:T(8,128)S(1)} fusion(f32[256,4,256]{2,0,1:T(8,128)} %bitcast.13, s32[1024]{0:T(1024)S(1)} %pad_clamp_fusion), kind=kCustom, calls=%fused_computation.2.clone | custom fusion | bytes 2097168 | tf_op jit(solution)/shard_map/jit(_take)/gather | solution.py:12
  75.9 1.3 bitcast_multiply_fusion.2
  77.1 1.6 %copy.12 = f32[256,4,256]{0,2,1:T(8,128)S(1)} copy(f32[256,4,256]{2,0,1:T(8,128)} %get-tuple-element.13) | data formatting | bytes 2097152 | tf_op jit(solution)/shard_map/mul | solution.py:34
  78.7 0.3 copy.10
  79.1 34.6 %reduce-scatter.2.cloned.1.call-done = f32[1,256,1024]{1,2,0:T(8,128)} async-done(((f32[8,256,1024]{1,2,0:T(8,128)}), f32[1,256,1024]{1,2,0:T(8,128)}) %reduce-scatter.2.cloned.1.call-update) | async-done | bytes 1048592 | tf_op jit(solution)/shard_map/reduce_scatter | solution.py:31
  113.6 4.2 %bitcast_subtract_fusion = (f32[256,1024]{0,1:T(8,128)}, f32[256,1024]{0,1:T(8,128)S(1)}, f32[256,1024]{0,1:T(8,128)}) fusion(f32[256,4,256]{0,2,1:T(8,128)} %copy.9, f32[1,256,1024]{1,2,0:T(8,128)} %reduce-scatter.2.cloned.1.call-done, f32[]{:T(128)} %convert_reduce_fusion, f32[256,4,256]{0,2,1:T(8,128)S(1)} %copy.12, f32[256,4,256]{0,2,1:T(8,128)S(1)} %copy.10), kind=kLoop, calls=%fused_computation.10 | loop fusion | flops 3145728 | bytes 7340036 | tf_op jit(solution)/shard_map/sub | solution.py:37
  117.8 2.5 %copy.13 = f32[256,1024]{1,0:T(8,128)} copy(f32[256,1024]{0,1:T(8,128)} %get-tuple-element.9) | data formatting | bytes 2097152
  120.4 2.5 %copy.14 = f32[256,1024]{1,0:T(8,128)} copy(f32[256,1024]{0,1:T(8,128)} %get-tuple-element.11) | data formatting | bytes 2097152
  122.9 1.3 copy.15
  (5 shorter events, 0.0 us)
Async XLA Ops:
  7.2 6.5 %copy-start.2 = (s32[8]{0:T(128)S(1)}, s32[8]{0:T(128)}, u32[]{:S(2)}) copy-start(s32[8]{0:T(128)} %param.13) | copy-start | bytes 100
  7.2 106.5 %reduce-scatter.2.cloned.1.call-start = ((), (), s32[]{:S(2)}) async-start(), calls=%async_computation.4 | async-start | bytes 9437184 | tf_op jit(solution)/shard_map/reduce_scatter | solution.py:31
  14.3 7.0 %copy-start = (f32[1024,256]{1,0:T(8,128)S(1)}, f32[1024,256]{1,0:T(8,128)}, u32[]{:S(2)}) copy-start(f32[1024,256]{1,0:T(8,128)} %param.8) | copy-start | bytes 3145732
  21.2 22.7 %copy-start.1 = (s32[1,4]{1,0:T(1,128)S(1)}, s32[1,4]{1,0:T(1,128)}, u32[]{:S(2)}) copy-start(s32[1,4]{1,0:T(1,128)} %param.12) | copy-start | bytes 52
  40.4 16.0 %all-to-all-start.1 = ((f32[4,256,256]{2,1,0:T(8,128)}), f32[4,256,256]{2,1,0:T(8,128)S(1)}, u32[]{:S(2)}, u32[]{:S(2)}) async-start(f32[4,256,256]{2,1,0:T(8,128)} %bitcast.5), calls=%async_computation.1 | async-start | bytes 2097152 | tf_op jit(solution)/shard_map/all_to_all | solution.py:19
  56.4 17.6 %all-to-all-start.2 = ((f32[4,256,256]{2,1,0:T(8,128)}), f32[4,256,256]{2,1,0:T(8,128)}, u32[]{:S(2)}, u32[]{:S(2)}) async-start(f32[4,256,256]{2,1,0:T(8,128)} %bitcast.12), calls=%async_computation.3 | async-start | bytes 2097152 | tf_op jit(solution)/shard_map/all_to_all | solution.py:20
Sparse Core Ops, SparseCore 0:
  21.4 92.2 reduce-scatter.1
where the time goes:
time: 132 us; the launch traced here: 131 us
  waiting for transfers between devices  56.3 us (43%)
  local copies, waits for them, and re-layouts  19.7 us (15%)
  blocking collectives  19.1 us (14%)
  between operations  14.2 us (11%)
  other arithmetic  13.9 us (11%)
  starting transfers between devices  7.81 us (6%)
    reduce_scatter x1, waiting for transfers between devices, body(): lax.psum_scatter(masked, 'dp', scatter_dimension=0, tiled=True)  34.6 us
    all_to_all x1, blocking collectives, body(): lax.all_to_all(old_weight, 'fsdp', split_axis=0, concat_axis=1, tiled=True)  19.1 us
    unnamed x10, local copies, waits for them, and re-layouts  12.9 us
    all_to_all x1, waiting for transfers between devices, body(): lax.all_to_all(old_first, 'fsdp', split_axis=0, concat_axis=1, tiled=True)  11.1 us
    all_to_all x1, waiting for transfers between devices, body(): lax.all_to_all(old_second, 'fsdp', split_axis=0, concat_axis=1, tiled=True)  10.5 us
    mul x1, other arithmetic, body(): masked = partial_grad.astype(jnp.float32) * own_live  6.93 us
    all_to_all x1, starting transfers between devices, body(): lax.all_to_all(old_second, 'fsdp', split_axis=0, concat_axis=1, tiled=True)  4.25 us
    sub x1, other arithmetic, body(): weight - 0.02 * (first_hat / (jnp.sqrt(second_corrected) + 1e-08) + 0.25...  4.17 us
  transfers between devices with their start and end apart: 3, of which 3 were waited for; matrix products, arithmetic and copies ran while one was open for 7% of the time, Pallas kernels for 0%

commit v1 on v0

v1 whole, which is shorter than its diff:
```python
import jax
import jax.numpy as jnp
from jax import lax
from jax.sharding import PartitionSpec as P

STEP = 1000


def restore_columns(block, lookup, shards):
    rows = block.shape[0] // shards
    pieces = [block[held * rows : (held + 1) * rows] for held in range(shards)]
    columns = []
    for place in range(shards):
        chosen = pieces[0]
        for held in range(1, shards):
            chosen = jnp.where(lookup[held] == place, pieces[held], chosen)
        columns.append(chosen)
    return jnp.concatenate(columns, axis=1)


def body(old_weight, old_first, old_second, grads, column_shard_lookup, alive):
    shards = lax.axis_size("fsdp")
    live_mask = alive.astype(jnp.float32)
    remaining_entries = jnp.sum(live_mask)
    own_live = lax.dynamic_index_in_dim(live_mask, lax.axis_index("dp"), 0, keepdims=False)
    partial_grad = grads[0].reshape(-1, grads.shape[3])
    masked = partial_grad.astype(jnp.float32) * own_live
    reduced_total = lax.psum_scatter(masked, "dp", scatter_dimension=0, tiled=True)
    lookup = column_shard_lookup[0]
    weight, first, second = [
        restore_columns(lax.all_to_all(state, "fsdp", split_axis=0, concat_axis=0, tiled=True), lookup, shards)
        for state in (old_weight, old_first, old_second)
    ]
    gradient_matrix = reduced_total / remaining_entries
    first_new = 0.9 * first + 0.1 * gradient_matrix
    second_new = 0.95 * second + 0.05 * gradient_matrix * gradient_matrix
    first_hat = first_new / (1.0 - 0.9**STEP)
    second_corrected = second_new / (1.0 - 0.95**STEP)
    weight_new = weight - 0.02 * (first_hat / (jnp.sqrt(second_corrected) + 1e-08) + 0.25 * weight)
    return (weight_new, first_new, second_new)


def solution(mesh):
    return jax.shard_map(
        body,
        mesh=mesh,
        in_specs=(
            P("dp", "fsdp"),
            P("dp", "fsdp"),
            P("dp", "fsdp"),
            P("dp", None, "fsdp", None),
            P("dp", None),
            P(),
        ),
        out_specs=(P(("dp", "fsdp"), None), P(("dp", "fsdp"), None), P(("dp", "fsdp"), None)),
        check_vma=False,
    )
```

time: 132 us -> 120 us (0.909)
  local copies, waits for them, and re-layouts: 19.7 us -> 1.19 us
  between operations: 14.2 us -> 21.9 us
  waiting for transfers between devices: 56.3 us -> 54.5 us
  other arithmetic: 13.9 us -> 15.6 us
    unnamed x10 -> x6, local copies, waits for them, and re-layouts: 12.9 us -> 0.01 us
    all_to_all x2, waiting for transfers between devices: 21.7 us -> 14.2 us  [body(): lax.all_to_all(state, 'fsdp', split_axis=0, concat_axis=0, tiled=True)]
    reduce_scatter x1, waiting for transfers between devices: 34.6 us -> 40.3 us  [body(): lax.psum_scatter(masked, 'dp', scatter_dimension=0, tiled=True)]
    gather x3 -> x0, local copies, waits for them, and re-layouts: 3.1 us -> none  [restore_columns(): jnp.take(pieces, column_order, axis=1).reshape(rows_here, block.shape[1])]
    select_n x2 -> x6, other arithmetic: 0.17 us -> 2.74 us  [restore_columns(): chosen = jnp.where(lookup[held] == place, pieces[held], chosen)]
    mul x2 -> x0, local copies, waits for them, and re-layouts: 1.89 us -> none  [the longest x1 1.56 us: body(): second_new = 0.95 * second + 0.05 * gradient_matrix * gradient_matrix]
  transfers between devices with their start and end apart: 3 -> 3, of which waited for: 3 -> 3; matrix products, arithmetic and copies ran while one was open for 7% -> 3% of each run, Pallas kernels for 0% -> 0%
where the time goes in v1:
time: 120 us; the launch traced here: 119 us
  waiting for transfers between devices  54.5 us (45%)
  between operations  21.9 us (18%)
  blocking collectives  19.1 us (16%)
  other arithmetic  15.6 us (13%)
  starting transfers between devices  7.07 us (6%)
    reduce_scatter x1, waiting for transfers between devices, body(): lax.psum_scatter(masked, 'dp', scatter_dimension=0, tiled=True)  40.3 us
    all_to_all x1, blocking collectives, body(): lax.all_to_all(state, 'fsdp', split_axis=0, concat_axis=0, tiled=True)  19.1 us
    all_to_all x2, waiting for transfers between devices, body(): lax.all_to_all(state, 'fsdp', split_axis=0, concat_axis=0, tiled=True)  14.2 us
    mul x1, other arithmetic, body(): masked = partial_grad.astype(jnp.float32) * own_live  7.34 us
    all_to_all x2, starting transfers between devices, body(): lax.all_to_all(state, 'fsdp', split_axis=0, concat_axis=0, tiled=True)  7.04 us
    sub x1, other arithmetic, body(): weight - 0.02 * (first_hat / (jnp.sqrt(second_corrected) + 1e-08) + 0.25...  4.32 us
    select_n x6, other arithmetic, restore_columns(): chosen = jnp.where(lookup[held] == place, pieces[held], chosen)  2.74 us
  transfers between devices with their start and end apart: 3, of which 3 were waited for; matrix products, arithmetic and copies ran while one was open for 3% of the time, Pallas kernels for 0%

profile of v1, /device:TPU:0, one launch (start us, length us, event | category | flops | bytes accessed | tf_op | source)
XLA Modules:
  0.0 119.4 jit_solution(1559879188327439834)
XLA Ops:
  7.2 0.0 reduce-scatter.2.cloned.1.call-start
  7.2 0.7 convert_element_type.8
  7.9 0.6 dynamic_slice.4
  8.5 0.0 copy-start
  8.5 7.3 %convert_multiply_fusion = f32[1,8,256,1024]{3,2,1,0:T(8,128)} fusion(bf16[1,8,256,1024]{3,2,1,0:T(8,128)(2,1)} %param.9, f32[]{:T(128)} %bitcast.22), kind=kLoop, calls=%fused_computation | loop fusion | flops 4194304 | bytes 12582916 | tf_op jit(solution)/shard_map/mul | solution.py:27
  15.8 0.0 copy-start.1
  15.8 0.0 copy-start.2
  15.8 0.0 reduce-scatter.2.cloned.1.call-update
  15.8 0.0 copy-done
  15.8 19.1 %all_to_all.27 = f32[4,256,256]{2,1,0:T(8,128)S(1)} all-to-all(f32[4,256,256]{2,1,0:T(8,128)S(1)} %bitcast.42), channel_id=1, replica_groups=mesh['dp'=8,'fsdp'=4] {'fsdp'}, dimensions={0} | all-to-all | bytes 2097152 | tf_op jit(solution)/shard_map/all_to_all | solution.py:31
  35.0 3.5 %all-to-all-start.2 = ((f32[4,256,256]{2,1,0:T(8,128)}), f32[4,256,256]{2,1,0:T(8,128)S(1)}, u32[]{:S(2)}, u32[]{:S(2)}) async-start(f32[4,256,256]{2,1,0:T(8,128)} %bitcast.24), calls=%async_computation.3 | async-start | bytes 2097152 | tf_op jit(solution)/shard_map/all_to_all | solution.py:31
  38.5 0.0 copy-done.1
  38.5 0.6 fusion.4
  46.9 0.0 copy-done.2
  46.9 0.6 convert_reduce_fusion
  47.5 3.5 %all-to-all-done.2 = f32[4,256,256]{2,1,0:T(8,128)S(1)} async-done(((f32[4,256,256]{2,1,0:T(8,128)}), f32[4,256,256]{2,1,0:T(8,128)S(1)}, u32[]{:S(2)}, u32[]{:S(2)}) %all-to-all-start.2) | async-done | bytes 1048608 | tf_op jit(solution)/shard_map/all_to_all | solution.py:31
  51.0 3.5 %all-to-all-start.1 = ((f32[4,256,256]{2,1,0:T(8,128)}), f32[4,256,256]{2,1,0:T(8,128)S(1)}, u32[]{:S(2)}, u32[]{:S(2)}) async-start(f32[4,256,256]{2,1,0:T(8,128)} %bitcast.43), calls=%async_computation.1 | async-start | bytes 2097152 | tf_op jit(solution)/shard_map/all_to_all | solution.py:31
  54.5 0.8 select_bitcast_fusion.9
  55.3 0.9 select_bitcast_fusion.1
  56.2 0.9 select_bitcast_fusion.11
  57.1 0.1 select_bitcast_fusion.3
  57.1 10.6 %all-to-all-done.1 = f32[4,256,256]{2,1,0:T(8,128)S(1)} async-done(((f32[4,256,256]{2,1,0:T(8,128)}), f32[4,256,256]{2,1,0:T(8,128)S(1)}, u32[]{:S(2)}, u32[]{:S(2)}) %all-to-all-start.1) | async-done | bytes 1048608 | tf_op jit(solution)/shard_map/all_to_all | solution.py:31
  67.7 0.1 select_bitcast_fusion.5
  67.8 0.1 select_bitcast_fusion.7
  67.9 40.3 %reduce-scatter.2.cloned.1.call-done = f32[256,1024]{1,0:T(8,128)} async-done(((f32[2048,1024]{1,0:T(8,128)}), f32[256,1024]{1,0:T(8,128)}) %reduce-scatter.2.cloned.1.call-update) | async-done | bytes 1048592 | tf_op jit(solution)/shard_map/reduce_scatter | solution.py:28
  108.2 4.3 %multiply_subtract_fusion = (f32[256,1024]{1,0:T(8,128)}, f32[256,1024]{1,0:T(8,128)}, f32[256,1024]{1,0:T(8,128)}) fusion(f32[256,256]{1,0:T(8,128)} %get-tuple-element.17, f32[256,256]{1,0:T(8,128)S(1)} %get-tuple-element.16, f32[256,256]{1,0:T(8,128)} %get-tuple-element.15, f32[256,256]{1,0:T(8,128)} %get-tuple-element.14, ...), kind=kLoop, calls=%fused_computation.7 | loop fusion | flops 6029312 | bytes 7340036 | tf_op jit(solution)/shard_map/sub | solution.py:39
Async XLA Ops:
  7.2 101.1 %reduce-scatter.2.cloned.1.call-start = ((), (), s32[]{:S(2)}) async-start(), calls=%async_computation.4 | async-start | bytes 9437184 | tf_op jit(solution)/shard_map/reduce_scatter | solution.py:28
  8.5 7.4 %copy-start = (f32[1024,256]{1,0:T(8,128)S(1)}, f32[1024,256]{1,0:T(8,128)}, u32[]{:S(2)}) copy-start(f32[1024,256]{1,0:T(8,128)} %param.6) | copy-start | bytes 3145732
  15.8 22.7 %copy-start.1 = (s32[1,4]{1,0:T(1,128)S(1)}, s32[1,4]{1,0:T(1,128)}, u32[]{:S(2)}) copy-start(s32[1,4]{1,0:T(1,128)} %param.10) | copy-start | bytes 52
  15.8 31.1 %copy-start.2 = (s32[8]{0:T(128)S(1)}, s32[8]{0:T(128)}, u32[]{:S(2)}) copy-start(s32[8]{0:T(128)} %param.11) | copy-start | bytes 100
  35.0 16.0 %all-to-all-start.2 = ((f32[4,256,256]{2,1,0:T(8,128)}), f32[4,256,256]{2,1,0:T(8,128)S(1)}, u32[]{:S(2)}, u32[]{:S(2)}) async-start(f32[4,256,256]{2,1,0:T(8,128)} %bitcast.24), calls=%async_computation.3 | async-start | bytes 2097152 | tf_op jit(solution)/shard_map/all_to_all | solution.py:31
  51.0 16.7 %all-to-all-start.1 = ((f32[4,256,256]{2,1,0:T(8,128)}), f32[4,256,256]{2,1,0:T(8,128)S(1)}, u32[]{:S(2)}, u32[]{:S(2)}) async-start(f32[4,256,256]{2,1,0:T(8,128)} %bitcast.43), calls=%async_computation.1 | async-start | bytes 2097152 | tf_op jit(solution)/shard_map/all_to_all | solution.py:31
Sparse Core Ops, SparseCore 0:
  15.9 92.2 reduce-scatter.1
